TPU v7x, 32 devices: a whole 2x2x4 slice. The times are simulated.
32 devices in a mesh: grp: 8 (over y, x, core), head: 4 (over z).
Axes of the slice: x: 2, y: 2, z: 4, core: 2. Of those that a mesh axis runs over, the one named last changes fastest.
Arguments:
- q_nope: bfloat16 [4, 64, 128, 128], P(None, 'grp', 'head'), may hold values from -6 to 6
- q_rope: bfloat16 [4, 64, 128, 64], P(None, 'grp', 'head'), may hold values from -512 to 512
- w_absorb_k: bfloat16 [128, 128, 512], P('head'), may hold values from -0.5 to 0.5
- w_absorb_v: bfloat16 [128, 512, 128], P('head'), may hold values from -0.25 to 0.25
- latent_cache: bfloat16 [64, 1024, 576], P(('grp', 'head')), may hold values from -4 to 4
- new_latent: bfloat16 [4, 64, 576], P(None, ('grp', 'head')), may hold values from -6 to 6
- lengths: int32 [64], replicated, may hold values from 128 to 1020, as said below
- moves: int32 [4, 1], P('head'), may hold values from 1 to 7
Outputs:
- attended: bfloat16 [4, 64, 128, 128], P(None, 'grp', 'head')
Inputs may be any that keep to these rules, and one draw needn't show every extreme that they name: lengths[r] counts the live rows of latent_cache[r]; its later rows up to 1024 are padding that no query reads.
All inputs are finite; a program needn't handle non-finite values.
Results may differ from a plain program's by a relative error of at most 0.0077.
Values may be sent and summed in bfloat16 or wider, within the bound.
A program may use at most 64 MiB of HBM per device.

v0:
```python
import math
import jax
import jax.numpy as jnp
from jax import lax
from jax.sharding import PartitionSpec as P

HEAD_DIM = 128
ROPE = 64
LATENT = 512
BLOCK = 128
yarn_gain = (0.1 * math.log(40.0) + 1.0) ** 2


def passed_along(value, axis, steps):
    count = lax.axis_size(axis)
    pairs = [(source, (source + steps) % count) for source in range(count)]
    return lax.ppermute(value, axis, pairs)


def attend(queries, stored, counts, recent, moment, window, score_scale):
    holders = queries.shape[0]
    head_count = queries.shape[1]
    capacity = stored.shape[1]
    longest = jnp.max(counts)
    passes = (longest + window - 1) // window
    positions = jnp.arange(window, dtype=jnp.int32)

    def score_tile(tile_index, buffer):
        begin_at = tile_index * window
        key_rows = lax.dynamic_slice_in_dim(stored, begin_at, window, 1)
        partial_value = (
            jnp.einsum("rhc,rtc->rht", queries, key_rows, preferred_element_type=jnp.float32)
            * score_scale
        )
        inside = (begin_at + positions)[None, None, :] < counts[:, None, None]
        partial_value = jnp.where(inside, partial_value, -jnp.inf)
        return lax.dynamic_update_slice_in_dim(buffer, partial_value, begin_at, 2)

    empty = jnp.full((holders, head_count, capacity), -jnp.inf, jnp.float32)
    scores = lax.fori_loop(0, passes, score_tile, empty)
    extra_scores = (
        jnp.einsum("rhc,rjc->rhj", queries, recent, preferred_element_type=jnp.float32)
        * score_scale
    )
    step_live = jnp.arange(recent.shape[1], dtype=jnp.int32) <= moment
    extra_scores = jnp.where(step_live[None, None, :], extra_scores, -jnp.inf)
    peak = jnp.maximum(jnp.max(scores, axis=2), jnp.max(extra_scores, axis=2))[:, :, None]
    spread = jnp.exp(scores - peak)
    spread_new = jnp.exp(extra_scores - peak)
    softmax_sum = jnp.sum(spread, axis=2, keepdims=True) + jnp.sum(
        spread_new, axis=2, keepdims=True
    )
    weights = (spread / softmax_sum).astype(jnp.bfloat16)
    weights_new = (spread_new / softmax_sum).astype(jnp.bfloat16)
    start_value = jnp.einsum(
        "rhj,rjl->rhl", weights_new, recent[:, :, :LATENT], preferred_element_type=jnp.float32
    )

    def value_tile(tile_index, summed):
        begin_at = tile_index * window
        key_rows = lax.dynamic_slice_in_dim(stored, begin_at, window, 1)[:, :, :LATENT]
        weight_tile = lax.dynamic_slice_in_dim(weights, begin_at, window, 2)
        return summed + jnp.einsum(
            "rht,rtl->rhl", weight_tile, key_rows, preferred_element_type=jnp.float32
        )

    return lax.fori_loop(0, passes, value_tile, start_value).astype(jnp.bfloat16)


def body(q_nope, q_rope, w_absorb_k, w_absorb_v, latent_cache, new_latent, lengths, moves):
    step_count = q_nope.shape[0]
    holders = latent_cache.shape[0]
    capacity = latent_cache.shape[1]
    entries = latent_cache.shape[2]
    movers = moves.shape[1]
    window = min(4 * BLOCK, capacity)
    score_scale = yarn_gain / math.sqrt(HEAD_DIM + ROPE)
    group_count = lax.axis_size("grp")
    column_count = lax.axis_size("head")
    bit_count = group_count.bit_length() - 1
    offsets = moves[0]
    group_here = lax.axis_index("grp")
    column_here = lax.axis_index("head")
    first_slot = (group_here * column_count + column_here) * holders
    counts = lax.dynamic_slice_in_dim(lengths, first_slot, holders)
    source = jnp.mod(group_here - offsets, group_count)
    moved_counts = lengths[
        (source * column_count + column_here) * holders + jnp.arange(movers, dtype=jnp.int32)
    ]
    stored = latent_cache
    recent = jnp.zeros((holders, step_count, entries), jnp.bfloat16)
    results = []
    for moment in range(step_count):
        if moment == 2:
            moving = (stored[:movers], recent[:movers])
            for level in range(bit_count):
                arrived = passed_along((moving[0], moving[1]), "grp", 1 << level)
                chosen = offsets >> level & 1 == 1
                moving = (
                    jnp.where(chosen[:, None, None], arrived[0], moving[0]),
                    jnp.where(chosen[:, None, None], arrived[1], moving[1]),
                )
            stored = jnp.concatenate([moving[0], stored[movers:]], axis=0)
            recent = jnp.concatenate([moving[1], recent[movers:]], axis=0)
            counts = jnp.concatenate([moved_counts, counts[movers:]], axis=0)
        q_latent = jnp.einsum(
            "rhd,hdl->rhl", q_nope[moment], w_absorb_k, preferred_element_type=jnp.float32
        ).astype(jnp.bfloat16)
        query_rows = jnp.concatenate([q_latent, q_rope[moment]], axis=2)
        owned_rows = lax.all_to_all(query_rows, "head", split_axis=0, concat_axis=1, tiled=True)
        fresh_rows = new_latent[moment]
        recent = recent.at[:, moment].set(fresh_rows)
        latent_out = attend(owned_rows, stored, counts, recent, moment, window, score_scale)
        gathered = lax.all_to_all(latent_out, "head", split_axis=1, concat_axis=0, tiled=True)
        results.append(
            jnp.einsum(
                "rhl,hld->rhd", gathered, w_absorb_v, preferred_element_type=jnp.float32
            ).astype(jnp.bfloat16)
        )
    return jnp.stack(results)


def solution(mesh):
    placed = (
        P(None, "grp", "head", None),
        P(None, "grp", "head", None),
        P("head", None, None),
        P("head", None, None),
        P(("grp", "head"), None, None),
        P(None, ("grp", "head"), None),
        P(),
        P("head", None),
    )
    return jax.shard_map(
        body, mesh=mesh, in_specs=placed, out_specs=P(None, "grp", "head", None), check_vma=False
    )
```

profile of v0, /device:TPU:10, one launch (start us, length us, event | category | flops | bytes accessed | tf_op | source)
XLA Modules:
  0.0 180.7 jit_solution(15612328909421631202)
XLA Ops:
  1.0 2.4 %slice.168 = bf16[1,1024,576]{1,2,0:T(8,128)(2,1)} slice(bf16[2,1024,576]{1,2,0:T(8,128)(2,1)} %param.36), slice={[0:1], [0:1024], [0:576]} | slice | bytes 2359296 | tf_op jit(solution)/shard_map/slice | solution.py:95
  3.4 1.6 collective-permute-start.3
  5.1 2.8 %fusion.41 = bf16[8,32,512]{2,0,1:T(8,128)(2,1)S(1)} fusion(bf16[32,128,512]{2,1,0:T(8,128)(2,1)} %param.34, bf16[1,8,32,128]{3,2,1,0:T(8,128)(2,1)S(1)} %get-tuple-element.598), kind=kOutput, calls=%fused_computation.61 | convolution fusion | flops 33685504 | bytes 4521984 | tf_op jit(solution)/shard_map/rhd,hdl->rhl/dot_general | solution.py:106
  8.7 5.3 %all-to-all-start.2 = ((bf16[8,32,576]{2,1,0:T(8,128)(2,1)}), bf16[8,32,576]{2,1,0:T(8,128)(2,1)S(1)}, u32[]{:S(2)}, u32[]{:S(2)}) async-start(bf16[8,32,576]{2,1,0:T(8,128)(2,1)} %copy.84), calls=%async_computation.2 | async-start | bytes 655360 | tf_op jit(solution)/shard_map/all_to_all | solution.py:110
  14.6 2.8 %fusion.42 = bf16[8,32,512]{2,0,1:T(8,128)(2,1)S(1)} fusion(bf16[32,128,512]{2,1,0:T(8,128)(2,1)} %param.34, bf16[1,8,32,128]{3,2,1,0:T(8,128)(2,1)S(1)} %get-tuple-element.597), kind=kOutput, calls=%fused_computation.62 | convolution fusion | flops 33685504 | bytes 4521984 | tf_op jit(solution)/shard_map/rhd,hdl->rhl/dot_general | solution.py:106
  17.4 3.0 %fusion.43 = bf16[8,32,512]{2,0,1:T(8,128)(2,1)S(1)} fusion(bf16[32,128,512]{2,1,0:T(8,128)(2,1)} %param.34, bf16[1,8,32,128]{3,2,1,0:T(8,128)(2,1)S(1)} %get-tuple-element.599), kind=kOutput, calls=%fused_computation.63 | convolution fusion | flops 33685504 | bytes 4521984 | tf_op jit(solution)/shard_map/rhd,hdl->rhl/dot_general | solution.py:106
  25.9 1.5 collective-permute-start.1
  30.5 3.1 %copy.79 = bf16[2,1024,576]{2,1,0:T(8,128)(2,1)S(1)} copy(bf16[2,1024,576]{1,2,0:T(8,128)(2,1)} %param.36) | data formatting | bytes 4718592 | tf_op jit(solution)/shard_map/while | solution.py:67
  33.6 1.7 copy.95
  35.4 1.7 copy.106
  38.5 5.1 %all-to-all-start = ((bf16[8,32,576]{2,1,0:T(8,128)(2,1)}), bf16[8,32,576]{2,1,0:T(8,128)(2,1)}, u32[]{:S(2)}, u32[]{:S(2)}) async-start(bf16[8,32,576]{2,1,0:T(8,128)(2,1)} %copy.73), calls=%async_computation | async-start | bytes 655360 | tf_op jit(solution)/shard_map/all_to_all | solution.py:110
  44.9 2.8 %while.94 = (s32[]{:T(128)}, f32[2,128,1024]{1,2,0:T(8,128)}, s32[]{:T(128)}, s32[2]{0:T(128)S(1)}, bf16[2,1024,576]{1,2,0:T(8,128)(2,1)}, /*index=5*/bf16[2,128...) while((s32[]{:T(128)}, f32[2,128,1024]{1,2,0:T(8,128)}, s32[]{:T(128)}, ...), condition=%wide.region_10.11_spmd.clone, body=%wide.region_9.10_spmd.clone.sunk | while | flops 151258624 | bytes 2006183 | solution.py:40
  44.9 2.8 %fusion.143 = f32[2,128,1024]{1,2,0:T(8,128)} fusion(f32[2,128,1024]{1,2,0:T(8,128)} %get-tuple-element.1027, s32[]{:T(128)S(6)} %select_n.188, bf16[2,128,576]{1,2,0:T(8,128)(2,1)S(1)} %get-tuple-element.1041, bf16[2,1024,576]{1,2,0:T(8,128)(2,1)} %get-tuple-element.1040, pred[2,512]{1,0:T(4,128)(4,1)S(1)} %broadcast_compare_fusion.9), kind=kOutput, calls=%fused_computation.31.clone.1 | convolution fusion | flops 151257088 | bytes 2000896 | tf_op jit(solution)/shard_map/while/body/rhc,rtc->rht/dot_general | solution.py:32
  47.7 3.1 %all-to-all-done = bf16[8,32,576]{2,1,0:T(8,128)(2,1)} async-done(((bf16[8,32,576]{2,1,0:T(8,128)(2,1)}), bf16[8,32,576]{2,1,0:T(8,128)(2,1)}, u32[]{:S(2)}, u32[]{:S(2)}) %all-to-all-start) | async-done | bytes 294944 | tf_op jit(solution)/shard_map/all_to_all | solution.py:110
  50.8 5.6 %all-to-all-start.4 = ((bf16[8,32,576]{2,1,0:T(8,128)(2,1)}), bf16[8,32,576]{2,1,0:T(8,128)(2,1)S(1)}, u32[]{:S(2)}, u32[]{:S(2)}) async-start(bf16[8,32,576]{2,1,0:T(8,128)(2,1)} %copy.95), calls=%async_computation.4 | async-start | bytes 655360 | tf_op jit(solution)/shard_map/all_to_all | solution.py:110
  59.4 2.9 %while.93 = (s32[]{:T(128)}, f32[2,128,1024]{1,2,0:T(8,128)}, s32[]{:T(128)}, s32[2]{0:T(128)S(1)}, bf16[2,1024,576]{1,2,0:T(8,128)(2,1)}, /*index=5*/bf16[2,128...) while((s32[]{:T(128)}, f32[2,128,1024]{1,2,0:T(8,128)}, s32[]{:T(128)}, ...), condition=%wide.region_2.3_spmd.clone, body=%wide.region_1.2_spmd.clone.sunk | while | flops 151258624 | bytes 2006183 | solution.py:40
  59.5 2.8 %fusion.140 = f32[2,128,1024]{1,2,0:T(8,128)} fusion(f32[2,128,1024]{1,2,0:T(8,128)} %get-tuple-element.1084, s32[]{:T(128)S(6)} %select_n.186, bf16[2,128,576]{1,2,0:T(8,128)(2,1)} %get-tuple-element.1098, bf16[2,1024,576]{1,2,0:T(8,128)(2,1)} %get-tuple-element.1097, pred[2,512]{1,0:T(4,128)(4,1)S(1)} %broadcast_compare_fusion.8), kind=kOutput, calls=%fused_computation.23.clone.1 | convolution fusion | flops 151257088 | bytes 2000896 | tf_op jit(solution)/shard_map/while/body/rhc,rtc->rht/dot_general | solution.py:32
  62.3 1.4 reduce_max.100
  65.1 1.4 fusion.53
  67.8 3.0 %broadcast_select_fusion = (bf16[1,1024,576]{1,2,0:T(8,128)(2,1)}, bf16[1,1024,576]{1,2,0:T(8,128)(2,1)}) fusion(bf16[1,1024,576]{1,2,0:T(8,128)(2,1)} %collective-permute-done.3, pred[]{:T(512)} %bitcast.33, bf16[2,1024,576]{1,2,0:T(8,128)(2,1)S(1)} %copy-done.4), kind=kLoop, calls=%fused_computation.57 | loop fusion | flops 589824 | bytes 5898241 | tf_op jit(solution)/shard_map/jit(_where)/select_n | solution.py:100
  70.7 4.4 %collective-permute-start.4 = (bf16[1,1024,576]{1,2,0:T(8,128)(2,1)}, bf16[1,1024,576]{1,2,0:T(8,128)(2,1)}, u32[]{:S(2)}, u32[]{:S(2)}) collective-permute-start(bf16[1,1024,576]{1,2,0:T(8,128)(2,1)} %get-tuple-element.594), channel_id=1, source_target_pairs={{0,8},{4,12},{8,16},{12,20},{16,24},{20,28},{24,0},{28,4},{1,9},{5... | collective-permute-start | bytes 3538952 | tf_op jit(solution)/shard_map/ppermute | solution.py:17
  76.4 1.4 reduce_max.98
  80.3 1.4 fusion.52
  82.6 5.4 %all-to-all-start.6 = ((bf16[8,32,576]{2,1,0:T(8,128)(2,1)}), bf16[8,32,576]{2,1,0:T(8,128)(2,1)}, u32[]{:S(2)}, u32[]{:S(2)}) async-start(bf16[8,32,576]{2,1,0:T(8,128)(2,1)} %copy.106), calls=%async_computation.6 | async-start | bytes 655360 | tf_op jit(solution)/shard_map/all_to_all | solution.py:110
  88.4 9.9 %collective-permute-done.4 = bf16[1,1024,576]{1,2,0:T(8,128)(2,1)} collective-permute-done((bf16[1,1024,576]{1,2,0:T(8,128)(2,1)}, bf16[1,1024,576]{1,2,0:T(8,128)(2,1)}, u32[]{:S(2)}, u32[]{:S(2)}) %collective-permute-start.4) | collective-permute-done | bytes 1179680 | tf_op jit(solution)/shard_map/ppermute | solution.py:17
  98.2 2.4 %broadcast_select_fusion.1 = bf16[1,1024,576]{1,2,0:T(8,128)(2,1)} fusion(bf16[1,1024,576]{1,2,0:T(8,128)(2,1)} %collective-permute-done.4, bf16[1,1024,576]{1,2,0:T(8,128)(2,1)} %get-tuple-element.594, pred[]{:T(512)} %bitcast.32), kind=kLoop, calls=%fused_computation.58 | loop fusion | flops 589824 | bytes 3538945 | tf_op jit(solution)/shard_map/jit(_where)/select_n | solution.py:100
  101.4 4.0 %all-to-all-start.3 = ((bf16[2,128,512]{2,0,1:T(2,128)(2,1)}), bf16[2,128,512]{2,0,1:T(2,128)(2,1)}, u32[]{:S(2)}, u32[]{:S(2)}) async-start(bf16[2,128,512]{2,0,1:T(2,128)(2,1)} %copy.154), calls=%async_computation.3 | async-start | bytes 524288 | tf_op jit(solution)/shard_map/all_to_all | solution.py:114
  105.4 1.4 while.89
  107.9 3.9 %all-to-all-done.3 = bf16[2,128,512]{2,0,1:T(2,128)(2,1)} async-done(((bf16[2,128,512]{2,0,1:T(2,128)(2,1)}), bf16[2,128,512]{2,0,1:T(2,128)(2,1)}, u32[]{:S(2)}, u32[]{:S(2)}) %all-to-all-start.3) | async-done | bytes 262176 | tf_op jit(solution)/shard_map/all_to_all | solution.py:114
  111.8 5.5 %all-to-all-start.1 = ((bf16[2,128,512]{2,0,1:T(2,128)(2,1)}), bf16[2,128,512]{2,0,1:T(2,128)(2,1)S(1)}, u32[]{:S(2)}, u32[]{:S(2)}) async-start(bf16[2,128,512]{2,0,1:T(2,128)(2,1)} %copy.155), calls=%async_computation.1 | async-start | bytes 524288 | tf_op jit(solution)/shard_map/all_to_all | solution.py:114
  121.9 1.7 all-to-all-done.1
  124.7 2.8 %fusion.45 = bf16[1,8,32,128]{3,1,2,0:T(8,128)(2,1)S(1)} fusion(bf16[8,32,512]{2,0,1:T(8,128)(2,1)S(1)} %all_to_all.119, bf16[32,512,128]{2,1,0:T(8,128)(2,1)} %param.35), kind=kOutput, calls=%fused_computation.69 | convolution fusion | flops 33587200 | bytes 4521984 | tf_op jit(solution)/shard_map/rhl,hld->rhd/dot_general | solution.py:116
  127.5 1.5 broadcast_select_fusion.2
  129.5 1.8 while.95
  129.6 1.6 fusion.146
  133.3 2.1 %while.96 = (s32[]{:T(128)}, f32[2,128,1024]{1,2,0:T(8,128)S(1)}, s32[]{:T(128)}, s32[2]{0:T(128)S(1)}, bf16[2,1024,576]{1,2,0:T(8,128)(2,1)}, /*index=5*/bf16[2...) while((s32[]{:T(128)}, f32[2,128,1024]{1,2,0:T(8,128)S(1)}, s32[]{:T(128)}, ...), condition=%wide.region_26.27_spmd.clone, body=%wide.region_25.26_spmd.clone.sunk | while | flops 151258624 | bytes 2007207 | solution.py:40
  133.4 2.0 %fusion.149 = f32[2,128,1024]{1,2,0:T(8,128)S(1)} fusion(f32[2,128,1024]{1,2,0:T(8,128)S(1)} %get-tuple-element.913, s32[]{:T(128)S(6)} %select_n.192, bf16[2,128,576]{1,2,0:T(8,128)(2,1)} %get-tuple-element.927, bf16[2,1024,576]{1,2,0:T(8,128)(2,1)} %get-tuple-element.926, pred[2,512]{1,0:T(4,128)(4,1)S(1)} %broadcast_compare_fusion.11), kind=kOutput, calls=%fused_computation.47.clone.1 | convolution fusion | flops 151257088 | bytes 2001920 | tf_op jit(solution)/shard_map/while/body/rhc,rtc->rht/dot_general | solution.py:32
  138.2 3.1 %copy.101 = bf16[2,1024,576]{2,1,0:T(8,128)(2,1)S(1)} copy(bf16[2,1024,576]{1,2,0:T(8,128)(2,1)} %get-tuple-element.1135) | data formatting | bytes 4718592 | tf_op jit(solution)/shard_map/while | solution.py:67
  141.3 2.2 %divide_convert_fusion.1 = bf16[2,128,1024]{1,2,0:T(8,128)(2,1)} fusion(f32[2,128,1024]{1,2,0:T(8,128)} %copy-done.3, f32[2,128]{1,0:T(2,128)S(1)} %add.192, f32[2,128]{1,0:T(2,128)S(1)} %max.30), kind=kLoop, calls=%fused_computation.82 | loop fusion | flops 786432 | bytes 1574912 | tf_op jit(solution)/shard_map/convert_element_type | solution.py:53
  143.5 2.3 %while.92 = (s32[]{:T(128)}, f32[2,128,512]{2,1,0:T(8,128)}, s32[]{:T(128)}, bf16[2,128,1024]{1,2,0:T(8,128)(2,1)}, bf16[2,1024,576]{2,1,0:T(8,128)(2,1)S(1)}, /*index=5*/s32[]{:T(128)}, s32[]{:T(128)}, s32[]{:T(128)}, s32[]{:T(128)}) while((s32[]{:T(128)}, f32[2,128,512]{2,1,0:T(8,128)}, s32[]{:T(128)}, bf16[2,128,1024]{1,2,0:T(8,128)(2,1)}, ...), condition=%wide.region_32.33_spmd, body=%wide.region_31.32_spmd.sunk | while | flops 134348800 | bytes 2360467 | solution.py:67
  143.5 2.3 %convolution_add_fusion.11 = f32[2,128,512]{2,1,0:T(8,128)} fusion(f32[2,128,512]{2,1,0:T(8,128)} %get-tuple-element.942, bf16[2,1024,576]{2,1,0:T(8,128)(2,1)S(1)} %get-tuple-element.954, s32[]{:T(128)S(6)} %select_n.184, bf16[2,128,1024]{1,2,0:T(8,128)(2,1)} %get-tuple-element.953), kind=kOutput, calls=%fused_computation.16.clone.1 | convolution fusion | flops 134348800 | bytes 2360320 | tf_op jit(solution)/shard_map/while/body/rht,rtl->rhl/dot_general | solution.py:63
  145.7 2.1 %copy.152 = bf16[2,128,512]{2,0,1:T(2,128)(2,1)} copy(f32[2,128,512]{2,1,0:T(8,128)} %get-tuple-element.324) | data formatting | bytes 786432 | tf_op jit(solution)/shard_map/while | solution.py:67
  147.9 11.7 %all-to-all-start.7 = ((bf16[2,128,512]{2,0,1:T(2,128)(2,1)}), bf16[2,128,512]{2,0,1:T(2,128)(2,1)}, u32[]{:S(2)}, u32[]{:S(2)}) async-start(bf16[2,128,512]{2,0,1:T(2,128)(2,1)} %copy.152), calls=%async_computation.7 | async-start | bytes 524288 | tf_op jit(solution)/shard_map/all_to_all | solution.py:114
  162.0 3.8 %all-to-all-done.7 = bf16[2,128,512]{2,0,1:T(2,128)(2,1)} async-done(((bf16[2,128,512]{2,0,1:T(2,128)(2,1)}), bf16[2,128,512]{2,0,1:T(2,128)(2,1)}, u32[]{:S(2)}, u32[]{:S(2)}) %all-to-all-start.7) | async-done | bytes 262176 | tf_op jit(solution)/shard_map/all_to_all | solution.py:114
  165.9 4.0 %all-to-all-start.5 = ((bf16[2,128,512]{2,0,1:T(2,128)(2,1)}), bf16[2,128,512]{2,0,1:T(2,128)(2,1)S(1)}, u32[]{:S(2)}, u32[]{:S(2)}) async-start(bf16[2,128,512]{2,0,1:T(2,128)(2,1)} %copy.153), calls=%async_computation.5 | async-start | bytes 524288 | tf_op jit(solution)/shard_map/all_to_all | solution.py:114
  169.9 2.8 %fusion.44 = bf16[1,8,32,128]{3,1,2,0:T(8,128)(2,1)S(1)} fusion(bf16[8,32,512]{2,0,1:T(8,128)(2,1)S(1)} %copy-done.11, bf16[32,512,128]{2,1,0:T(8,128)(2,1)} %param.35), kind=kOutput, calls=%fused_computation.68 | convolution fusion | flops 33587200 | bytes 4521984 | tf_op jit(solution)/shard_map/rhl,hld->rhd/dot_general | solution.py:116
  173.9 2.8 %fusion.47 = bf16[1,8,32,128]{3,1,2,0:T(8,128)(2,1)S(1)} fusion(bf16[8,32,512]{2,0,1:T(8,128)(2,1)S(1)} %all_to_all.135, bf16[32,512,128]{2,1,0:T(8,128)(2,1)} %param.35), kind=kOutput, calls=%fused_computation.71 | convolution fusion | flops 33587200 | bytes 4521984 | tf_op jit(solution)/shard_map/rhl,hld->rhd/dot_general | solution.py:116
  177.1 2.8 %fusion.46 = bf16[1,8,32,128]{3,1,2,0:T(8,128)(2,1)S(1)} fusion(bf16[8,32,512]{2,0,1:T(8,128)(2,1)S(1)} %all_to_all.127, bf16[32,512,128]{2,1,0:T(8,128)(2,1)} %param.35), kind=kOutput, calls=%fused_computation.70 | convolution fusion | flops 33587200 | bytes 4521984 | tf_op jit(solution)/shard_map/rhl,hld->rhd/dot_general | solution.py:116
  (143 shorter events, 43.3 us)
Async XLA Ops:
  0.0 5.0 %copy-start.12 = (bf16[4,8,32,64]{3,2,1,0:T(8,128)(2,1)S(1)}, bf16[4,8,32,64]{3,2,1,0:T(8,128)(2,1)}, u32[]{:S(2)}) copy-start(bf16[4,8,32,64]{3,2,1,0:T(8,128)(2,1)} %param.33) | copy-start | bytes 393220
  0.0 5.0 %copy-start.13 = (bf16[4,8,32,128]{3,2,1,0:T(8,128)(2,1)S(1)}, bf16[4,8,32,128]{3,2,1,0:T(8,128)(2,1)}, u32[]{:S(2)}) copy-start(bf16[4,8,32,128]{3,2,1,0:T(8,128)(2,1)} %param.32) | copy-start | bytes 786436
  0.9 24.9 %collective-permute-start = (bf16[1,4,576]{2,1,0:T(4,128)(2,1)S(1)}, bf16[1,4,576]{2,1,0:T(4,128)(2,1)S(1)}, u32[]{:S(2)}, u32[]{:S(2)}) collective-permute-start(bf16[1,4,576]{2,1,0:T(4,128)(2,1)S(1)} %slice.181), channel_id=1, source_target_pairs={{0,4},{4,8},{8,12},{12,16},{16,20},{20,24},{24,28},{28,0},{1,5},{5... | collective-permute-start | bytes 13832 | tf_op jit(solution)/shard_map/ppermute | solution.py:17
  3.4 64.4 %collective-permute-start.3 = (bf16[1,1024,576]{1,2,0:T(8,128)(2,1)}, bf16[1,1024,576]{1,2,0:T(8,128)(2,1)}, u32[]{:S(2)}, u32[]{:S(2)}) collective-permute-start(bf16[1,1024,576]{1,2,0:T(8,128)(2,1)} %slice.168), channel_id=1, source_target_pairs={{0,4},{4,8},{8,12},{12,16},{16,20},{20,24},{24,28},{28,0},{1,5},{5... | collective-permute-start | bytes 3538952 | tf_op jit(solution)/shard_map/ppermute | solution.py:17
  8.7 29.7 %all-to-all-start.2 = ((bf16[8,32,576]{2,1,0:T(8,128)(2,1)}), bf16[8,32,576]{2,1,0:T(8,128)(2,1)S(1)}, u32[]{:S(2)}, u32[]{:S(2)}) async-start(bf16[8,32,576]{2,1,0:T(8,128)(2,1)} %copy.84), calls=%async_computation.2 | async-start | bytes 655360 | tf_op jit(solution)/shard_map/all_to_all | solution.py:110
  17.4 3.5 %copy-start = (bf16[32,128,512]{2,1,0:T(8,128)(2,1)S(1)}, bf16[32,128,512]{2,1,0:T(8,128)(2,1)}, u32[]{:S(2)}) copy-start(bf16[32,128,512]{2,1,0:T(8,128)(2,1)} %param.34) | copy-start | bytes 12582916
  20.9 2.3 %copy-start.14 = (s32[64]{0:T(128)S(1)}, s32[64]{0:T(128)}, u32[]{:S(2)}) copy-start(s32[64]{0:T(128)} %param.38) | copy-start | bytes 772
  25.9 12.0 %collective-permute-start.1 = (bf16[1,4,576]{2,1,0:T(4,128)(2,1)S(1)}, bf16[1,4,576]{2,1,0:T(4,128)(2,1)S(1)}, u32[]{:S(2)}, u32[]{:S(2)}) collective-permute-start(bf16[1,4,576]{2,1,0:T(4,128)(2,1)S(1)} %get-tuple-element.608), channel_id=1, source_target_pairs={{0,8},{4,12},{8,16},{12,20},{16,24},{20,28},{24,0},{28,4},{1,9},{5... | collective-permute-start | bytes 13832 | tf_op jit(solution)/shard_map/ppermute | solution.py:17
  37.9 79.5 %collective-permute-start.2 = (bf16[1,4,576]{2,1,0:T(4,128)(2,1)S(1)}, bf16[1,4,576]{2,1,0:T(4,128)(2,1)S(1)}, u32[]{:S(2)}, u32[]{:S(2)}) collective-permute-start(bf16[1,4,576]{2,1,0:T(4,128)(2,1)S(1)} %broadcast_select_fusion.4), channel_id=1, source_target_pairs={{0,16},{4,20},{8,24},{12,28},{16,0},{20,4},{24,8},{28,12},{1,17},{... | collective-permute-start | bytes 13832 | tf_op jit(solution)/shard_map/ppermute | solution.py:17
  38.5 12.4 %all-to-all-start = ((bf16[8,32,576]{2,1,0:T(8,128)(2,1)}), bf16[8,32,576]{2,1,0:T(8,128)(2,1)}, u32[]{:S(2)}, u32[]{:S(2)}) async-start(bf16[8,32,576]{2,1,0:T(8,128)(2,1)} %copy.73), calls=%async_computation | async-start | bytes 655360 | tf_op jit(solution)/shard_map/all_to_all | solution.py:110
  43.6 1.3 copy-start.10
  50.8 31.8 %all-to-all-start.4 = ((bf16[8,32,576]{2,1,0:T(8,128)(2,1)}), bf16[8,32,576]{2,1,0:T(8,128)(2,1)S(1)}, u32[]{:S(2)}, u32[]{:S(2)}) async-start(bf16[8,32,576]{2,1,0:T(8,128)(2,1)} %copy.95), calls=%async_computation.4 | async-start | bytes 655360 | tf_op jit(solution)/shard_map/all_to_all | solution.py:110
  57.4 2.0 %copy-start.9 = (bf16[4,2,32,576]{3,2,0,1:T(8,128)(2,1)}, bf16[4,2,32,576]{3,2,0,1:T(8,128)(2,1)S(1)}, u32[]{:S(2)}) copy-start(bf16[4,2,32,576]{3,2,0,1:T(8,128)(2,1)S(1)} %copy.74) | copy-start | bytes 884740
  59.4 4.3 %copy-start.15 = (pred[4]{0:T(512)(128)(4,1)S(1)}, pred[4]{0:T(512)(128)(4,1)}, u32[]{:S(2)}) copy-start(pred[4]{0:T(512)(128)(4,1)} %iota_compare_fusion.2) | copy-start | bytes 16
  63.7 3.1 %copy-start.1 = (f32[2,128,1024]{1,2,0:T(8,128)S(1)}, f32[2,128,1024]{1,2,0:T(8,128)}, u32[]{:S(2)}) copy-start(f32[2,128,1024]{1,2,0:T(8,128)} %get-tuple-element.319) | copy-start | bytes 3145732
  63.7 4.1 %copy-start.4 = (bf16[2,1024,576]{1,2,0:T(8,128)(2,1)S(1)}, bf16[2,1024,576]{1,2,0:T(8,128)(2,1)}, u32[]{:S(2)}) copy-start(bf16[2,1024,576]{1,2,0:T(8,128)(2,1)} %get-tuple-element.1133) | copy-start | bytes 7077892
  70.7 27.5 %collective-permute-start.4 = (bf16[1,1024,576]{1,2,0:T(8,128)(2,1)}, bf16[1,1024,576]{1,2,0:T(8,128)(2,1)}, u32[]{:S(2)}, u32[]{:S(2)}) collective-permute-start(bf16[1,1024,576]{1,2,0:T(8,128)(2,1)} %get-tuple-element.594), channel_id=1, source_target_pairs={{0,8},{4,12},{8,16},{12,20},{16,24},{20,28},{24,0},{28,4},{1,9},{5... | collective-permute-start | bytes 3538952 | tf_op jit(solution)/shard_map/ppermute | solution.py:17
  77.8 3.8 %copy-start.2 = (f32[2,128,1024]{1,2,0:T(8,128)S(1)}, f32[2,128,1024]{1,2,0:T(8,128)}, u32[]{:S(2)}) copy-start(f32[2,128,1024]{1,2,0:T(8,128)} %get-tuple-element.317) | copy-start | bytes 3145732
  82.6 18.7 %all-to-all-start.6 = ((bf16[8,32,576]{2,1,0:T(8,128)(2,1)}), bf16[8,32,576]{2,1,0:T(8,128)(2,1)}, u32[]{:S(2)}, u32[]{:S(2)}) async-start(bf16[8,32,576]{2,1,0:T(8,128)(2,1)} %copy.106), calls=%async_computation.6 | async-start | bytes 655360 | tf_op jit(solution)/shard_map/all_to_all | solution.py:110
  100.7 26.9 %collective-permute-start.5 = (bf16[1,1024,576]{1,2,0:T(8,128)(2,1)}, bf16[1,1024,576]{1,2,0:T(8,128)(2,1)}, u32[]{:S(2)}, u32[]{:S(2)}) collective-permute-start(bf16[1,1024,576]{1,2,0:T(8,128)(2,1)} %broadcast_select_fusion.1), channel_id=1, source_target_pairs={{0,16},{4,20},{8,24},{12,28},{16,0},{20,4},{24,8},{28,12},{1,17},{... | collective-permute-start | bytes 3538952 | tf_op jit(solution)/shard_map/ppermute | solution.py:17
  101.4 10.4 %all-to-all-start.3 = ((bf16[2,128,512]{2,0,1:T(2,128)(2,1)}), bf16[2,128,512]{2,0,1:T(2,128)(2,1)}, u32[]{:S(2)}, u32[]{:S(2)}) async-start(bf16[2,128,512]{2,0,1:T(2,128)(2,1)} %copy.154), calls=%async_computation.3 | async-start | bytes 524288 | tf_op jit(solution)/shard_map/all_to_all | solution.py:114
  111.8 11.9 %all-to-all-start.1 = ((bf16[2,128,512]{2,0,1:T(2,128)(2,1)}), bf16[2,128,512]{2,0,1:T(2,128)(2,1)S(1)}, u32[]{:S(2)}, u32[]{:S(2)}) async-start(bf16[2,128,512]{2,0,1:T(2,128)(2,1)} %copy.155), calls=%async_computation.1 | async-start | bytes 524288 | tf_op jit(solution)/shard_map/all_to_all | solution.py:114
  119.6 7.9 %copy-start.7 = (bf16[4,2,32,576]{3,2,0,1:T(8,128)(2,1)}, bf16[4,2,32,576]{3,2,0,1:T(8,128)(2,1)S(1)}, u32[]{:S(2)}) copy-start(bf16[4,2,32,576]{3,2,0,1:T(8,128)(2,1)S(1)} %copy.107) | copy-start | bytes 884740
  127.5 1.6 copy-start.6
  131.2 1.0 copy-start.3
  131.2 1.7 copy-start.5
  133.3 2.2 %copy-start.8 = (bf16[4,2,32,576]{3,2,0,1:T(8,128)(2,1)S(1)}, bf16[4,2,32,576]{3,2,0,1:T(8,128)(2,1)}, u32[]{:S(2)}) copy-start(bf16[4,2,32,576]{3,2,0,1:T(8,128)(2,1)} %copy-done.7) | copy-start | bytes 884740
  147.9 18.0 %all-to-all-start.7 = ((bf16[2,128,512]{2,0,1:T(2,128)(2,1)}), bf16[2,128,512]{2,0,1:T(2,128)(2,1)}, u32[]{:S(2)}, u32[]{:S(2)}) async-start(bf16[2,128,512]{2,0,1:T(2,128)(2,1)} %copy.152), calls=%async_computation.7 | async-start | bytes 524288 | tf_op jit(solution)/shard_map/all_to_all | solution.py:114
  159.5 10.3 %copy-start.11 = (bf16[8,32,512]{2,0,1:T(8,128)(2,1)S(1)}, bf16[8,32,512]{2,0,1:T(8,128)(2,1)}, u32[]{:S(2)}) copy-start(bf16[8,32,512]{2,0,1:T(8,128)(2,1)} %all_to_all.111) | copy-start | bytes 786436
  165.9 10.9 %all-to-all-start.5 = ((bf16[2,128,512]{2,0,1:T(2,128)(2,1)}), bf16[2,128,512]{2,0,1:T(2,128)(2,1)S(1)}, u32[]{:S(2)}, u32[]{:S(2)}) async-start(bf16[2,128,512]{2,0,1:T(2,128)(2,1)} %copy.153), calls=%async_computation.5 | async-start | bytes 524288 | tf_op jit(solution)/shard_map/all_to_all | solution.py:114
where the time goes:
time: 183 us; the launch traced here: 181 us
  starting transfers between devices  55.5 us (30%)
  matrix products  41.1 us (22%)
  local copies, waits for them, and re-layouts  35.3 us (19%)
  other arithmetic  23 us (13%)
  waiting for transfers between devices  22.5 us (12%)
  between operations  3.04 us (2%)
    all_to_all x4, starting transfers between devices, body(): lax.all_to_all(latent_out, 'head', split_axis=1, concat_axis=0, tiled=True)  25.2 us
    all_to_all x4, starting transfers between devices, body(): lax.all_to_all(query_rows, 'head', split_axis=0, concat_axis=1, tiled=True)  21.5 us
    while x6, local copies, waits for them, and re-layouts, attend(): lax.fori_loop(0, passes, value_tile, start_value).astype(jnp.bfloat16)  11.7 us
    dot_general x4, matrix products, body(): jnp.einsum('rhl,hld->rhd', gathered, w_absorb_v, preferred_element_type=j...  11.3 us
    ppermute x6, waiting for transfers between devices, passed_along(): return lax.ppermute(value, axis, pairs)  9.89 us
    all_to_all x4, waiting for transfers between devices, body(): lax.all_to_all(latent_out, 'head', split_axis=1, concat_axis=0, tiled=True)  9.49 us
    dot_general x4, matrix products, body(): jnp.einsum('rhd,hdl->rhl', q_nope[moment], w_absorb_k, preferred_element_...  9.29 us
    dot_general x4, matrix products, score_tile(): jnp.einsum('rhc,rtc->rht', queries, key_rows, preferred_element_type=jnp....  9.25 us
  transfers between devices with their start and end apart: 14, of which 5 were waited for; matrix products, arithmetic and copies ran while one was open for 40% of the time, Pallas kernels for 0%

commit v1 on v0

--- a/solution.py
+++ b/solution.py
@@ -9,6 +9,12 @@
 LATENT = 512
 BLOCK = 128
 yarn_gain = (0.1 * math.log(40.0) + 1.0) ** 2
+
+
+def stacked_exchange(x, axis, split, join):
+    parts = jnp.split(x, lax.axis_size(axis), axis=split)
+    received = lax.all_to_all(jnp.stack(parts), axis, 0, 0)
+    return jnp.concatenate(received, axis=join)
 
 
 def passed_along(value, axis, steps):
@@ -111,7 +117,7 @@
         fresh_rows = new_latent[moment]
         recent = recent.at[:, moment].set(fresh_rows)
         latent_out = attend(owned_rows, stored, counts, recent, moment, window, score_scale)
-        gathered = lax.all_to_all(latent_out, "head", split_axis=1, concat_axis=0, tiled=True)
+        gathered = stacked_exchange(latent_out, "head", 1, 0)
         results.append(
             jnp.einsum(
                 "rhl,hld->rhd", gathered, w_absorb_v, preferred_element_type=jnp.float32

time: 183 us -> 191 us (1.044)
  the two profiles are of different devices: /device:TPU:10 before, /device:TPU:0 now
where the time goes in v1:
time: 191 us; the launch traced here: 189 us
  starting transfers between devices  68.3 us (36%)
  matrix products  37.8 us (20%)
  other arithmetic  28.6 us (15%)
  local copies, waits for them, and re-layouts  27.7 us (15%)
  waiting for transfers between devices  22.9 us (12%)
  between operations  3.03 us (2%)
    all_to_all x4, starting transfers between devices, stacked_exchange(): received = lax.all_to_all(jnp.stack(parts), axis, 0, 0)  31.4 us
    all_to_all x4, starting transfers between devices, body(): lax.all_to_all(query_rows, 'head', split_axis=0, concat_axis=1, tiled=True)  27 us
    all_to_all x4, waiting for transfers between devices, stacked_exchange(): received = lax.all_to_all(jnp.stack(parts), axis, 0, 0)  12.9 us
    ppermute x6, waiting for transfers between devices, passed_along(): return lax.ppermute(value, axis, pairs)  9.97 us
    ppermute x6, starting transfers between devices, passed_along(): return lax.ppermute(value, axis, pairs)  9.92 us
    dot_general x4, matrix products, body(): jnp.einsum('rhl,hld->rhd', gathered, w_absorb_v, preferred_element_type=j...  9.66 us
    dot_general x4, matrix products, score_tile(): jnp.einsum('rhc,rtc->rht', queries, key_rows, preferred_element_type=jnp....  9.22 us
    dot_general x4, matrix products, value_tile(): jnp.einsum('rht,rtl->rhl', weight_tile, key_rows, preferred_element_type=...  7.19 us
  transfers between devices with their start and end apart: 14, of which 6 were waited for; matrix products, arithmetic and copies ran while one was open for 46% of the time, Pallas kernels for 0%

profile of v1, /device:TPU:0, one launch (start us, length us, event | category | flops | bytes accessed | tf_op | source)
XLA Modules:
  0.0 188.5 jit_solution(1445391300458256755)
XLA Ops:
  1.5 2.4 %slice.168 = bf16[1,1024,576]{1,2,0:T(8,128)(2,1)} slice(bf16[2,1024,576]{1,2,0:T(8,128)(2,1)} %param.36), slice={[0:1], [0:1024], [0:576]} | slice | bytes 2359296 | tf_op jit(solution)/shard_map/slice | solution.py:101
  3.8 2.6 %collective-permute-start.3 = (bf16[1,1024,576]{1,2,0:T(8,128)(2,1)}, bf16[1,1024,576]{1,2,0:T(8,128)(2,1)}, u32[]{:S(2)}, u32[]{:S(2)}) collective-permute-start(bf16[1,1024,576]{1,2,0:T(8,128)(2,1)} %slice.168), channel_id=1, source_target_pairs={{0,4},{4,8},{8,12},{12,16},{16,20},{20,24},{24,28},{28,0},{1,5},{5... | collective-permute-start | bytes 3538952 | tf_op jit(solution)/shard_map/ppermute | solution.py:23
  6.6 2.8 %fusion.41 = bf16[8,32,512]{2,0,1:T(8,128)(2,1)S(1)} fusion(bf16[32,128,512]{2,1,0:T(8,128)(2,1)} %param.34, bf16[1,8,32,128]{3,2,1,0:T(8,128)(2,1)S(1)} %get-tuple-element.602), kind=kOutput, calls=%fused_computation.61 | convolution fusion | flops 33685504 | bytes 4521984 | tf_op jit(solution)/shard_map/rhd,hdl->rhl/dot_general | solution.py:112
  10.2 4.9 %all-to-all-start.2 = ((bf16[8,32,576]{2,1,0:T(8,128)(2,1)}), bf16[8,32,576]{2,1,0:T(8,128)(2,1)S(1)}, u32[]{:S(2)}, u32[]{:S(2)}) async-start(bf16[8,32,576]{2,1,0:T(8,128)(2,1)} %copy.83), calls=%async_computation.2 | async-start | bytes 655360 | tf_op jit(solution)/shard_map/all_to_all | solution.py:116
  15.1 3.0 %fusion.42 = bf16[8,32,512]{2,0,1:T(8,128)(2,1)S(1)} fusion(bf16[32,128,512]{2,1,0:T(8,128)(2,1)} %param.34, bf16[1,8,32,128]{3,2,1,0:T(8,128)(2,1)S(1)} %get-tuple-element.601), kind=kOutput, calls=%fused_computation.62 | convolution fusion | flops 33685504 | bytes 4521984 | tf_op jit(solution)/shard_map/rhd,hdl->rhl/dot_general | solution.py:112
  22.1 1.5 collective-permute-start.1
  26.7 1.6 collective-permute-start.2
  31.5 3.1 %copy.79 = bf16[2,1024,576]{2,1,0:T(8,128)(2,1)S(1)} copy(bf16[2,1024,576]{1,2,0:T(8,128)(2,1)} %param.36) | data formatting | bytes 4718592 | tf_op jit(solution)/shard_map/while | solution.py:73
  34.6 1.7 copy.93
  36.3 1.7 copy.103
  38.9 5.1 %all-to-all-start = ((bf16[8,32,576]{2,1,0:T(8,128)(2,1)}), bf16[8,32,576]{2,1,0:T(8,128)(2,1)S(1)}, u32[]{:S(2)}, u32[]{:S(2)}) async-start(bf16[8,32,576]{2,1,0:T(8,128)(2,1)} %copy.73), calls=%async_computation | async-start | bytes 655360 | tf_op jit(solution)/shard_map/all_to_all | solution.py:116
  48.2 2.8 %while.94 = (s32[]{:T(128)}, f32[2,128,1024]{1,2,0:T(8,128)}, s32[]{:T(128)}, s32[2]{0:T(128)S(1)}, bf16[2,1024,576]{1,2,0:T(8,128)(2,1)}, /*index=5*/bf16[2,128...) while((s32[]{:T(128)}, f32[2,128,1024]{1,2,0:T(8,128)}, s32[]{:T(128)}, ...), condition=%wide.region_10.11_spmd.clone, body=%wide.region_9.10_spmd.clone.sunk | while | flops 151258624 | bytes 2006183 | solution.py:46
  48.3 2.8 %fusion.143 = f32[2,128,1024]{1,2,0:T(8,128)} fusion(f32[2,128,1024]{1,2,0:T(8,128)} %get-tuple-element.1043, s32[]{:T(128)S(6)} %select_n.188, bf16[2,128,576]{1,2,0:T(8,128)(2,1)S(1)} %get-tuple-element.1057, bf16[2,1024,576]{1,2,0:T(8,128)(2,1)} %get-tuple-element.1056, pred[2,512]{1,0:T(4,128)(4,1)S(1)} %broadcast_compare_fusion.9), kind=kOutput, calls=%fused_computation.31.clone.1 | convolution fusion | flops 151257088 | bytes 2000896 | tf_op jit(solution)/shard_map/while/body/rhc,rtc->rht/dot_general | solution.py:38
  51.1 1.4 reduce_max.100
  52.5 1.4 fusion.53
  53.9 2.2 %divide_convert_fusion.2 = bf16[2,128,1024]{1,2,0:T(8,128)(2,1)} fusion(f32[2,128,1024]{1,2,0:T(8,128)} %get-tuple-element.319, f32[2,128]{1,0:T(2,128)S(1)} %add.187, f32[2,128]{1,0:T(2,128)S(1)} %max.29), kind=kLoop, calls=%fused_computation.84 | loop fusion | flops 786432 | bytes 1574912 | tf_op jit(solution)/shard_map/convert_element_type | solution.py:59
  56.8 7.9 %all-to-all-start.4 = ((bf16[8,32,576]{2,1,0:T(8,128)(2,1)}), bf16[8,32,576]{2,1,0:T(8,128)(2,1)S(1)}, u32[]{:S(2)}, u32[]{:S(2)}) async-start(bf16[8,32,576]{2,1,0:T(8,128)(2,1)} %copy.93), calls=%async_computation.4 | async-start | bytes 655360 | tf_op jit(solution)/shard_map/all_to_all | solution.py:116
  67.9 2.9 %while.93 = (s32[]{:T(128)}, f32[2,128,1024]{1,2,0:T(8,128)}, s32[]{:T(128)}, s32[2]{0:T(128)S(1)}, bf16[2,1024,576]{1,2,0:T(8,128)(2,1)}, /*index=5*/bf16[2,128...) while((s32[]{:T(128)}, f32[2,128,1024]{1,2,0:T(8,128)}, s32[]{:T(128)}, ...), condition=%wide.region_2.3_spmd.clone, body=%wide.region_1.2_spmd.clone.sunk | while | flops 151258624 | bytes 2006183 | solution.py:46
  68.0 2.8 %fusion.140 = f32[2,128,1024]{1,2,0:T(8,128)} fusion(f32[2,128,1024]{1,2,0:T(8,128)} %get-tuple-element.1100, s32[]{:T(128)S(6)} %select_n.186, bf16[2,128,576]{1,2,0:T(8,128)(2,1)} %get-tuple-element.1114, bf16[2,1024,576]{1,2,0:T(8,128)(2,1)} %get-tuple-element.1113, pred[2,512]{1,0:T(4,128)(4,1)S(1)} %broadcast_compare_fusion.8), kind=kOutput, calls=%fused_computation.23.clone.1 | convolution fusion | flops 151257088 | bytes 2000896 | tf_op jit(solution)/shard_map/while/body/rhc,rtc->rht/dot_general | solution.py:38
  70.8 1.4 reduce_max.98
  72.2 1.4 fusion.52
  73.6 2.2 %divide_convert_fusion.3 = bf16[2,128,1024]{1,2,0:T(8,128)(2,1)} fusion(f32[2,128,1024]{1,2,0:T(8,128)} %get-tuple-element.317, f32[2,128]{1,0:T(2,128)S(1)} %add.186, f32[2,128]{1,0:T(2,128)S(1)} %max.28), kind=kLoop, calls=%fused_computation.86 | loop fusion | flops 786432 | bytes 1574912 | tf_op jit(solution)/shard_map/convert_element_type | solution.py:59
  77.4 3.6 %broadcast_select_fusion = (bf16[1,1024,576]{1,2,0:T(8,128)(2,1)}, bf16[1,1024,576]{1,2,0:T(8,128)(2,1)}) fusion(bf16[1,1024,576]{1,2,0:T(8,128)(2,1)} %collective-permute-done.3, pred[]{:T(512)} %bitcast.39, bf16[2,1024,576]{1,2,0:T(8,128)(2,1)} %get-tuple-element.1149), kind=kLoop, calls=%fused_computation.57 | loop fusion | flops 589824 | bytes 5898241 | tf_op jit(solution)/shard_map/jit(_where)/select_n | solution.py:106
  81.0 2.2 %collective-permute-start.4 = (bf16[1,1024,576]{1,2,0:T(8,128)(2,1)}, bf16[1,1024,576]{1,2,0:T(8,128)(2,1)}, u32[]{:S(2)}, u32[]{:S(2)}) collective-permute-start(bf16[1,1024,576]{1,2,0:T(8,128)(2,1)} %get-tuple-element.594), channel_id=1, source_target_pairs={{0,8},{4,12},{8,16},{12,20},{16,24},{20,28},{24,0},{28,4},{1,9},{5... | collective-permute-start | bytes 3538952 | tf_op jit(solution)/shard_map/ppermute | solution.py:23
  84.3 2.3 %while.89 = (s32[]{:T(128)}, f32[2,128,512]{2,1,0:T(8,128)}, s32[]{:T(128)}, bf16[2,128,1024]{1,2,0:T(8,128)(2,1)}, bf16[2,1024,576]{2,1,0:T(8,128)(2,1)S(1)}, /*index=5*/s32[]{:T(128)}, s32[]{:T(128)}, s32[]{:T(128)}, s32[]{:T(128)}) while((s32[]{:T(128)}, f32[2,128,512]{2,1,0:T(8,128)}, s32[]{:T(128)}, bf16[2,128,1024]{1,2,0:T(8,128)(2,1)}, ...), condition=%wide.region_8.9_spmd, body=%wide.region_7.8_spmd.sunk | while | flops 134348800 | bytes 2360467 | solution.py:73
  84.3 2.3 %convolution_add_fusion.8 = f32[2,128,512]{2,1,0:T(8,128)} fusion(f32[2,128,512]{2,1,0:T(8,128)} %get-tuple-element.1129, bf16[2,1024,576]{2,1,0:T(8,128)(2,1)S(1)} %get-tuple-element.1141, s32[]{:T(128)S(6)} %select_n.181, bf16[2,128,1024]{1,2,0:T(8,128)(2,1)} %get-tuple-element.1140), kind=kOutput, calls=%fused_computation.4.clone.1 | convolution fusion | flops 134348800 | bytes 2360320 | tf_op jit(solution)/shard_map/while/body/rht,rtl->rhl/dot_general | solution.py:69
  87.7 9.1 %all-to-all-start.6 = ((bf16[8,32,576]{2,1,0:T(8,128)(2,1)}), bf16[8,32,576]{2,1,0:T(8,128)(2,1)S(1)}, u32[]{:S(2)}, u32[]{:S(2)}) async-start(bf16[8,32,576]{2,1,0:T(8,128)(2,1)} %copy.103), calls=%async_computation.6 | async-start | bytes 655360 | tf_op jit(solution)/shard_map/all_to_all | solution.py:116
  96.8 8.8 %collective-permute-done.4 = bf16[1,1024,576]{1,2,0:T(8,128)(2,1)} collective-permute-done((bf16[1,1024,576]{1,2,0:T(8,128)(2,1)}, bf16[1,1024,576]{1,2,0:T(8,128)(2,1)}, u32[]{:S(2)}, u32[]{:S(2)}) %collective-permute-start.4) | collective-permute-done | bytes 1179680 | tf_op jit(solution)/shard_map/ppermute | solution.py:23
  105.6 1.4 broadcast_select_fusion.1
  107.0 1.5 collective-permute-start.5
  109.2 7.7 %all-to-all-start.3 = ((bf16[4,2,32,512]{3,2,1,0:T(8,128)(2,1)}), bf16[4,2,32,512]{3,2,1,0:T(8,128)(2,1)S(1)}, u32[]{:S(2)}, u32[]{:S(2)}) async-start(bf16[4,2,32,512]{3,2,1,0:T(8,128)(2,1)} %pad_maximum_fusion.6), calls=%async_computation.3 | async-start | bytes 524288 | tf_op jit(solution)/shard_map/all_to_all | solution.py:16
  119.8 3.9 %all-to-all-done.3 = bf16[4,2,32,512]{3,2,1,0:T(8,128)(2,1)S(1)} async-done(((bf16[4,2,32,512]{3,2,1,0:T(8,128)(2,1)}), bf16[4,2,32,512]{3,2,1,0:T(8,128)(2,1)S(1)}, u32[]{:S(2)}, u32[]{:S(2)}) %all-to-all-start.3) | async-done | bytes 262176 | tf_op jit(solution)/shard_map/all_to_all | solution.py:16
  123.7 4.0 %all-to-all-start.1 = ((bf16[4,2,32,512]{3,2,1,0:T(8,128)(2,1)}), bf16[4,2,32,512]{3,2,1,0:T(8,128)(2,1)}, u32[]{:S(2)}, u32[]{:S(2)}) async-start(bf16[4,2,32,512]{3,2,1,0:T(8,128)(2,1)} %pad_maximum_fusion.5), calls=%async_computation.1 | async-start | bytes 524288 | tf_op jit(solution)/shard_map/all_to_all | solution.py:16
  127.8 2.9 %fusion.45 = bf16[1,8,32,128]{3,1,2,0:T(8,128)(2,1)S(1)} fusion(bf16[32,512,128]{2,1,0:T(8,128)(2,1)} %param.35, bf16[8,32,512]{2,1,0:T(8,128)(2,1)S(1)} %bitcast.180), kind=kOutput, calls=%fused_computation.69 | convolution fusion | flops 33587200 | bytes 4521984 | tf_op jit(solution)/shard_map/rhl,hld->rhd/dot_general | solution.py:122
  130.8 1.5 broadcast_select_fusion.2
  132.6 1.9 %while.95 = (s32[]{:T(128)}, f32[2,128,1024]{1,2,0:T(8,128)S(1)}, s32[]{:T(128)}, s32[2]{0:T(128)S(1)}, bf16[2,1024,576]{1,2,0:T(8,128)(2,1)S(1)}, /*index=5*/bf...) while((s32[]{:T(128)}, f32[2,128,1024]{1,2,0:T(8,128)S(1)}, ...), condition=%wide.region_18.19_spmd.clone, body=%wide.region_17.18_spmd.clone.sunk | while | flops 151258624 | bytes 2007207 | solution.py:46
  132.7 1.6 fusion.146
  136.7 2.1 %while.96 = (s32[]{:T(128)}, f32[2,128,1024]{1,2,0:T(8,128)S(1)}, s32[]{:T(128)}, s32[2]{0:T(128)S(1)}, bf16[2,1024,576]{1,2,0:T(8,128)(2,1)}, /*index=5*/bf16[2...) while((s32[]{:T(128)}, f32[2,128,1024]{1,2,0:T(8,128)S(1)}, s32[]{:T(128)}, ...), condition=%wide.region_26.27_spmd.clone, body=%wide.region_25.26_spmd.clone.sunk | while | flops 151258624 | bytes 2007207 | solution.py:46
  136.8 2.0 %fusion.149 = f32[2,128,1024]{1,2,0:T(8,128)S(1)} fusion(f32[2,128,1024]{1,2,0:T(8,128)S(1)} %get-tuple-element.929, s32[]{:T(128)S(6)} %select_n.192, bf16[2,128,576]{1,2,0:T(8,128)(2,1)} %get-tuple-element.943, bf16[2,1024,576]{1,2,0:T(8,128)(2,1)} %get-tuple-element.942, pred[2,512]{1,0:T(4,128)(4,1)S(1)} %broadcast_compare_fusion.11), kind=kOutput, calls=%fused_computation.47.clone.1 | convolution fusion | flops 151257088 | bytes 2001920 | tf_op jit(solution)/shard_map/while/body/rhc,rtc->rht/dot_general | solution.py:38
  141.5 3.1 %copy.99 = bf16[2,1024,576]{2,1,0:T(8,128)(2,1)S(1)} copy(bf16[2,1024,576]{1,2,0:T(8,128)(2,1)} %get-tuple-element.1151) | data formatting | bytes 4718592 | tf_op jit(solution)/shard_map/while | solution.py:73
  144.6 2.3 %while.92 = (s32[]{:T(128)}, f32[2,128,512]{2,1,0:T(8,128)}, s32[]{:T(128)}, bf16[2,128,1024]{1,2,0:T(8,128)(2,1)}, bf16[2,1024,576]{2,1,0:T(8,128)(2,1)S(1)}, /*index=5*/s32[]{:T(128)}, s32[]{:T(128)}, s32[]{:T(128)}, s32[]{:T(128)}) while((s32[]{:T(128)}, f32[2,128,512]{2,1,0:T(8,128)}, s32[]{:T(128)}, bf16[2,128,1024]{1,2,0:T(8,128)(2,1)}, ...), condition=%wide.region_32.33_spmd, body=%wide.region_31.32_spmd.sunk | while | flops 134348800 | bytes 2360467 | solution.py:73
  144.6 2.3 %convolution_add_fusion.11 = f32[2,128,512]{2,1,0:T(8,128)} fusion(f32[2,128,512]{2,1,0:T(8,128)} %get-tuple-element.958, bf16[2,1024,576]{2,1,0:T(8,128)(2,1)S(1)} %get-tuple-element.970, s32[]{:T(128)S(6)} %select_n.184, bf16[2,128,1024]{1,2,0:T(8,128)(2,1)} %get-tuple-element.969), kind=kOutput, calls=%fused_computation.16.clone.1 | convolution fusion | flops 134348800 | bytes 2360320 | tf_op jit(solution)/shard_map/while/body/rht,rtl->rhl/dot_general | solution.py:69
  149.8 15.5 %all-to-all-start.7 = ((bf16[4,2,32,512]{3,2,1,0:T(8,128)(2,1)}), bf16[4,2,32,512]{3,2,1,0:T(8,128)(2,1)S(1)}, u32[]{:S(2)}, u32[]{:S(2)}) async-start(bf16[4,2,32,512]{3,2,1,0:T(8,128)(2,1)} %pad_maximum_fusion.8), calls=%async_computation.7 | async-start | bytes 524288 | tf_op jit(solution)/shard_map/all_to_all | solution.py:16
  167.5 6.5 %all-to-all-done.7 = bf16[4,2,32,512]{3,2,1,0:T(8,128)(2,1)S(1)} async-done(((bf16[4,2,32,512]{3,2,1,0:T(8,128)(2,1)}), bf16[4,2,32,512]{3,2,1,0:T(8,128)(2,1)S(1)}, u32[]{:S(2)}, u32[]{:S(2)}) %all-to-all-start.7) | async-done | bytes 262176 | tf_op jit(solution)/shard_map/all_to_all | solution.py:16
  174.0 4.1 %all-to-all-start.5 = ((bf16[4,2,32,512]{3,2,1,0:T(8,128)(2,1)}), bf16[4,2,32,512]{3,2,1,0:T(8,128)(2,1)S(1)}, u32[]{:S(2)}, u32[]{:S(2)}) async-start(bf16[4,2,32,512]{3,2,1,0:T(8,128)(2,1)} %pad_maximum_fusion.7), calls=%async_computation.5 | async-start | bytes 524288 | tf_op jit(solution)/shard_map/all_to_all | solution.py:16
  178.1 3.1 %fusion.44 = bf16[1,8,32,128]{3,1,2,0:T(8,128)(2,1)S(1)} fusion(bf16[32,512,128]{2,1,0:T(8,128)(2,1)} %param.35, bf16[8,32,512]{2,1,0:T(8,128)(2,1)} %bitcast.12), kind=kOutput, calls=%fused_computation.68 | convolution fusion | flops 33587200 | bytes 4521984 | tf_op jit(solution)/shard_map/rhl,hld->rhd/dot_general | solution.py:122
  182.3 2.5 %all-to-all-done.5 = bf16[4,2,32,512]{3,2,1,0:T(8,128)(2,1)S(1)} async-done(((bf16[4,2,32,512]{3,2,1,0:T(8,128)(2,1)}), bf16[4,2,32,512]{3,2,1,0:T(8,128)(2,1)S(1)}, u32[]{:S(2)}, u32[]{:S(2)}) %all-to-all-start.5) | async-done | bytes 262176 | tf_op jit(solution)/shard_map/all_to_all | solution.py:16
  184.8 2.9 %fusion.46 = bf16[1,8,32,128]{3,1,2,0:T(8,128)(2,1)S(1)} fusion(bf16[32,512,128]{2,1,0:T(8,128)(2,1)} %param.35, bf16[8,32,512]{2,1,0:T(8,128)(2,1)S(1)} %bitcast.181), kind=kOutput, calls=%fused_computation.70 | convolution fusion | flops 33587200 | bytes 4521984 | tf_op jit(solution)/shard_map/rhl,hld->rhd/dot_general | solution.py:122
  (135 shorter events, 41.5 us)
Async XLA Ops:
  0.0 6.4 %copy-start.9 = (bf16[4,8,32,64]{3,2,1,0:T(8,128)(2,1)S(1)}, bf16[4,8,32,64]{3,2,1,0:T(8,128)(2,1)}, u32[]{:S(2)}) copy-start(bf16[4,8,32,64]{3,2,1,0:T(8,128)(2,1)} %param.33) | copy-start | bytes 393220
  0.0 6.5 %copy-start.10 = (bf16[4,8,32,128]{3,2,1,0:T(8,128)(2,1)S(1)}, bf16[4,8,32,128]{3,2,1,0:T(8,128)(2,1)}, u32[]{:S(2)}) copy-start(bf16[4,8,32,128]{3,2,1,0:T(8,128)(2,1)} %param.32) | copy-start | bytes 786436
  0.9 21.2 %collective-permute-start = (bf16[1,4,576]{2,1,0:T(4,128)(2,1)S(1)}, bf16[1,4,576]{2,1,0:T(4,128)(2,1)S(1)}, u32[]{:S(2)}, u32[]{:S(2)}) collective-permute-start(bf16[1,4,576]{2,1,0:T(4,128)(2,1)S(1)} %slice.181), channel_id=1, source_target_pairs={{0,4},{4,8},{8,12},{12,16},{16,20},{20,24},{24,28},{28,0},{1,5},{5... | collective-permute-start | bytes 13832 | tf_op jit(solution)/shard_map/ppermute | solution.py:23
  3.8 73.6 %collective-permute-start.3 = (bf16[1,1024,576]{1,2,0:T(8,128)(2,1)}, bf16[1,1024,576]{1,2,0:T(8,128)(2,1)}, u32[]{:S(2)}, u32[]{:S(2)}) collective-permute-start(bf16[1,1024,576]{1,2,0:T(8,128)(2,1)} %slice.168), channel_id=1, source_target_pairs={{0,4},{4,8},{8,12},{12,16},{16,20},{20,24},{24,28},{28,0},{1,5},{5... | collective-permute-start | bytes 3538952 | tf_op jit(solution)/shard_map/ppermute | solution.py:23
  10.2 28.7 %all-to-all-start.2 = ((bf16[8,32,576]{2,1,0:T(8,128)(2,1)}), bf16[8,32,576]{2,1,0:T(8,128)(2,1)S(1)}, u32[]{:S(2)}, u32[]{:S(2)}) async-start(bf16[8,32,576]{2,1,0:T(8,128)(2,1)} %copy.83), calls=%async_computation.2 | async-start | bytes 655360 | tf_op jit(solution)/shard_map/all_to_all | solution.py:116
  15.1 3.4 %copy-start = (bf16[32,128,512]{2,1,0:T(8,128)(2,1)S(1)}, bf16[32,128,512]{2,1,0:T(8,128)(2,1)}, u32[]{:S(2)}) copy-start(bf16[32,128,512]{2,1,0:T(8,128)(2,1)} %param.34) | copy-start | bytes 12582916
  19.2 4.5 %copy-start.11 = (s32[64]{0:T(128)S(1)}, s32[64]{0:T(128)}, u32[]{:S(2)}) copy-start(s32[64]{0:T(128)} %param.38) | copy-start | bytes 772
  22.1 4.6 %collective-permute-start.1 = (bf16[1,4,576]{2,1,0:T(4,128)(2,1)S(1)}, bf16[1,4,576]{2,1,0:T(4,128)(2,1)S(1)}, u32[]{:S(2)}, u32[]{:S(2)}) collective-permute-start(bf16[1,4,576]{2,1,0:T(4,128)(2,1)S(1)} %get-tuple-element.624), channel_id=1, source_target_pairs={{0,8},{4,12},{8,16},{12,20},{16,24},{20,28},{24,0},{28,4},{1,9},{5... | collective-permute-start | bytes 13832 | tf_op jit(solution)/shard_map/ppermute | solution.py:23
  26.7 12.1 %collective-permute-start.2 = (bf16[1,4,576]{2,1,0:T(4,128)(2,1)S(1)}, bf16[1,4,576]{2,1,0:T(4,128)(2,1)S(1)}, u32[]{:S(2)}, u32[]{:S(2)}) collective-permute-start(bf16[1,4,576]{2,1,0:T(4,128)(2,1)S(1)} %broadcast_select_fusion.4), channel_id=1, source_target_pairs={{0,16},{4,20},{8,24},{12,28},{16,0},{20,4},{24,8},{28,12},{1,17},{... | collective-permute-start | bytes 13832 | tf_op jit(solution)/shard_map/ppermute | solution.py:23
  38.9 17.1 %all-to-all-start = ((bf16[8,32,576]{2,1,0:T(8,128)(2,1)}), bf16[8,32,576]{2,1,0:T(8,128)(2,1)S(1)}, u32[]{:S(2)}, u32[]{:S(2)}) async-start(bf16[8,32,576]{2,1,0:T(8,128)(2,1)} %copy.73), calls=%async_computation | async-start | bytes 655360 | tf_op jit(solution)/shard_map/all_to_all | solution.py:116
  56.1 0.7 copy-start.8
  56.8 30.9 %all-to-all-start.4 = ((bf16[8,32,576]{2,1,0:T(8,128)(2,1)}), bf16[8,32,576]{2,1,0:T(8,128)(2,1)S(1)}, u32[]{:S(2)}, u32[]{:S(2)}) async-start(bf16[8,32,576]{2,1,0:T(8,128)(2,1)} %copy.93), calls=%async_computation.4 | async-start | bytes 655360 | tf_op jit(solution)/shard_map/all_to_all | solution.py:116
  81.0 24.6 %collective-permute-start.4 = (bf16[1,1024,576]{1,2,0:T(8,128)(2,1)}, bf16[1,1024,576]{1,2,0:T(8,128)(2,1)}, u32[]{:S(2)}, u32[]{:S(2)}) collective-permute-start(bf16[1,1024,576]{1,2,0:T(8,128)(2,1)} %get-tuple-element.594), channel_id=1, source_target_pairs={{0,8},{4,12},{8,16},{12,20},{16,24},{20,28},{24,0},{28,4},{1,9},{5... | collective-permute-start | bytes 3538952 | tf_op jit(solution)/shard_map/ppermute | solution.py:23
  87.7 21.5 %all-to-all-start.6 = ((bf16[8,32,576]{2,1,0:T(8,128)(2,1)}), bf16[8,32,576]{2,1,0:T(8,128)(2,1)S(1)}, u32[]{:S(2)}, u32[]{:S(2)}) async-start(bf16[8,32,576]{2,1,0:T(8,128)(2,1)} %copy.103), calls=%async_computation.6 | async-start | bytes 655360 | tf_op jit(solution)/shard_map/all_to_all | solution.py:116
  107.0 23.8 %collective-permute-start.5 = (bf16[1,1024,576]{1,2,0:T(8,128)(2,1)S(1)}, bf16[1,1024,576]{1,2,0:T(8,128)(2,1)}, u32[]{:S(2)}, u32[]{:S(2)}) collective-permute-start(bf16[1,1024,576]{1,2,0:T(8,128)(2,1)S(1)} %broadcast_select_fusion.1), channel_id=1, source_target_pairs={{0,16},{4,20},{8,24},{12,28},{16,0},{20,4},{24,8},{28,12},{1,17},{... | collective-permute-start | bytes 3538952 | tf_op jit(solution)/shard_map/ppermute | solution.py:23
  109.2 14.5 %all-to-all-start.3 = ((bf16[4,2,32,512]{3,2,1,0:T(8,128)(2,1)}), bf16[4,2,32,512]{3,2,1,0:T(8,128)(2,1)S(1)}, u32[]{:S(2)}, u32[]{:S(2)}) async-start(bf16[4,2,32,512]{3,2,1,0:T(8,128)(2,1)} %pad_maximum_fusion.6), calls=%async_computation.3 | async-start | bytes 524288 | tf_op jit(solution)/shard_map/all_to_all | solution.py:16
  117.9 12.7 %copy-start.6 = (bf16[4,2,32,576]{3,2,0,1:T(8,128)(2,1)}, bf16[4,2,32,576]{3,2,0,1:T(8,128)(2,1)S(1)}, u32[]{:S(2)}) copy-start(bf16[4,2,32,576]{3,2,0,1:T(8,128)(2,1)S(1)} %copy.104) | copy-start | bytes 884740
  123.7 26.1 %all-to-all-start.1 = ((bf16[4,2,32,512]{3,2,1,0:T(8,128)(2,1)}), bf16[4,2,32,512]{3,2,1,0:T(8,128)(2,1)}, u32[]{:S(2)}, u32[]{:S(2)}) async-start(bf16[4,2,32,512]{3,2,1,0:T(8,128)(2,1)} %pad_maximum_fusion.5), calls=%async_computation.1 | async-start | bytes 524288 | tf_op jit(solution)/shard_map/all_to_all | solution.py:16
  130.7 1.6 copy-start.5
  134.6 1.0 copy-start.2
  134.6 1.7 copy-start.4
  136.7 2.2 %copy-start.7 = (bf16[4,2,32,576]{3,2,0,1:T(8,128)(2,1)S(1)}, bf16[4,2,32,576]{3,2,0,1:T(8,128)(2,1)}, u32[]{:S(2)}) copy-start(bf16[4,2,32,576]{3,2,0,1:T(8,128)(2,1)} %copy-done.6) | copy-start | bytes 884740
  146.9 1.9 %copy-start.3 = (f32[2,128,1024]{1,2,0:T(8,128)S(1)}, f32[2,128,1024]{1,2,0:T(8,128)}, u32[]{:S(2)}) copy-start(f32[2,128,1024]{1,2,0:T(8,128)} %copy-done.2) | copy-start | bytes 3145732
  149.8 24.1 %all-to-all-start.7 = ((bf16[4,2,32,512]{3,2,1,0:T(8,128)(2,1)}), bf16[4,2,32,512]{3,2,1,0:T(8,128)(2,1)S(1)}, u32[]{:S(2)}, u32[]{:S(2)}) async-start(bf16[4,2,32,512]{3,2,1,0:T(8,128)(2,1)} %pad_maximum_fusion.8), calls=%async_computation.7 | async-start | bytes 524288 | tf_op jit(solution)/shard_map/all_to_all | solution.py:16
  174.0 10.9 %all-to-all-start.5 = ((bf16[4,2,32,512]{3,2,1,0:T(8,128)(2,1)}), bf16[4,2,32,512]{3,2,1,0:T(8,128)(2,1)S(1)}, u32[]{:S(2)}, u32[]{:S(2)}) async-start(bf16[4,2,32,512]{3,2,1,0:T(8,128)(2,1)} %pad_maximum_fusion.7), calls=%async_computation.5 | async-start | bytes 524288 | tf_op jit(solution)/shard_map/all_to_all | solution.py:16
  178.1 3.5 %copy-start.1 = (bf16[32,512,128]{2,1,0:T(8,128)(2,1)S(1)}, bf16[32,512,128]{2,1,0:T(8,128)(2,1)}, u32[]{:S(2)}) copy-start(bf16[32,512,128]{2,1,0:T(8,128)(2,1)} %param.35) | copy-start | bytes 12582916
